TPU v7x, 128 devices: a whole 4x4x4 slice. The times are simulated.
128 devices in a mesh: req: 64 (over z, y, x), kv: 2 (over core).
Axes of the slice: x: 4, y: 4, z: 4, core: 2. Of those that a mesh axis runs over, the one named last changes fastest.
Arguments:
- queries: bfloat16 [16384, 2048], P(('req', 'kv')), may hold values from -6 to 6
- keys: bfloat16 [16384, 1024], P(('req', 'kv')), may hold values from -6 to 6
- values: bfloat16 [16384, 1024], P(('req', 'kv')), may hold values from -6 to 6
- residual: bfloat16 [16384, 3584], P(('req', 'kv'))
- segment_ids: int32 [16384], P(('req', 'kv')), may hold values from 127 to 16383, as said below
- regroup: int32 [16384], P(('req', 'kv')), may hold values from 0 to 16383, as said below
- out_weight: bfloat16 [2048, 3584], P('kv')
- attn_gain: float32 [3584], replicated, may hold values from 0.1 to 1.9
- pre_gain: float32 [3584], replicated, may hold values from 0.1 to 1.9
- gate_weight: bfloat16 [3584, 7168], P(None, 'kv'), may hold values from -0.09375 to 0.09375
- up_weight: bfloat16 [3584, 7168], P(None, 'kv'), may hold values from -0.09375 to 0.09375
- down_weight: bfloat16 [7168, 3584], P('kv')
- post_gain: float32 [3584], replicated, may hold values from 0.1 to 1.9
Outputs:
- layer_out: bfloat16 [16384, 3584], P(('req', 'kv'))
- key_cache_rows: bfloat16 [4, 16384, 256], P(None, ('req', 'kv'))
- value_cache_rows: bfloat16 [4, 16384, 256], P(None, ('req', 'kv'))
Inputs may be any that keep to these rules, and one draw needn't show every extreme that they name: `segment_ids`: A request is a run of consecutive slots carrying one id, the index of its last slot; no request runs from one index of req's 256 slots into the next. `regroup`: A permutation of the slots. Each device (in req+kv order) sends exactly one of its 128 slots to each of the 128 devices: for every pair of devices, exactly one slot of the first has its output row among the 128 rows of the second.
All inputs are finite; a program needn't handle non-finite values.
Results may differ from a plain program's by a relative error of at most 0.0095.
Values may be sent and summed in bfloat16 or wider, within the bound.
A program may use at most 192 MiB of HBM per device.

v0:
```python
import jax
import jax.numpy as jnp
from jax import lax
from jax.sharding import PartitionSpec as P

QUERY_HEADS = 8
KEY_VALUE_HEADS = 4
HEAD_ENTRIES = 256
WINDOW_REACH = 512
cap_value = 50.0
norm_eps = 1e-06


def from_behind(block, axis, distance):
    devices = range(lax.axis_size(axis))
    route = [(i - distance, i) for i in devices if i - distance in devices]
    return lax.ppermute(block, axis, route)


def rms_scale(values_in, gain_row):
    mean_square = jnp.mean(values_in * values_in, axis=-1, keepdims=True)
    return values_in * lax.rsqrt(mean_square + norm_eps) * gain_row


def key_mask(own_ids, key_ids, key_pos):
    distance = jnp.arange(own_ids.shape[0], dtype=jnp.int32)[:, None] - key_pos[None, :]
    return (own_ids[:, None] == key_ids[None, :]) & (distance >= 0) & (distance < WINDOW_REACH)


def block_terms(query_head_rows, key_heads, value_heads, allowed):
    raw_scores = jnp.einsum(
        "tkgd,skd->kgts", query_head_rows, key_heads, preferred_element_type=jnp.float32
    )
    scores = cap_value * jnp.tanh(raw_scores * HEAD_ENTRIES ** (-0.5) / cap_value)
    weights = jnp.where(allowed, jnp.exp(scores), 0.0)
    totals = jnp.sum(weights, axis=-1)
    numerator = jnp.einsum(
        "kgts,skd->tkgd",
        weights.astype(jnp.bfloat16),
        value_heads,
        preferred_element_type=jnp.float32,
    )
    return (numerator, totals)


def send_rows(normed_part, normed_pos, stream_part, key_portion, value_portion):
    received = (
        lax.all_to_all(normed_part, ("req", "kv"), split_axis=0, concat_axis=0, tiled=True),
        lax.all_to_all(normed_pos, ("req", "kv"), split_axis=0, concat_axis=0, tiled=True),
        lax.all_to_all(stream_part, ("req", "kv"), split_axis=0, concat_axis=0, tiled=True),
        lax.all_to_all(key_portion, ("req", "kv"), split_axis=0, concat_axis=0, tiled=True),
        lax.all_to_all(value_portion, ("req", "kv"), split_axis=0, concat_axis=0, tiled=True),
    )
    return received


def per_device(
    queries,
    keys,
    values,
    residual,
    segment_ids,
    regroup,
    out_weight,
    attn_gain,
    pre_gain,
    gate_weight,
    up_weight,
    down_weight,
    post_gain,
):
    resident_rows = queries.shape[0]
    grouped_heads = QUERY_HEADS // KEY_VALUE_HEADS
    query_head_rows = queries.reshape(resident_rows, KEY_VALUE_HEADS, grouped_heads, HEAD_ENTRIES)
    own_ids = segment_ids + 1
    base_pos = jnp.arange(resident_rows, dtype=jnp.int32)
    key_collections = [(keys, values, own_ids, base_pos)]
    moved_keys, moved_values, moved_ids = from_behind((keys, values, own_ids), "kv", 1)
    key_collections.append((moved_keys, moved_values, moved_ids, base_pos - resident_rows))
    gathered_keys = jnp.concatenate(
        [key_collection[0] for key_collection in key_collections], axis=0
    ).reshape(-1, KEY_VALUE_HEADS, HEAD_ENTRIES)
    gathered_values = jnp.concatenate(
        [key_collection[1] for key_collection in key_collections], axis=0
    ).reshape(-1, KEY_VALUE_HEADS, HEAD_ENTRIES)
    all_ids = jnp.concatenate([key_collection[2] for key_collection in key_collections], axis=0)
    all_pos = jnp.concatenate([key_collection[3] for key_collection in key_collections], axis=0)
    numerator, totals = block_terms(
        query_head_rows, gathered_keys, gathered_values, key_mask(own_ids, all_ids, all_pos)
    )
    attended_output = (
        (numerator / jnp.transpose(totals, (2, 0, 1))[..., None])
        .astype(jnp.bfloat16)
        .reshape(resident_rows, QUERY_HEADS * HEAD_ENTRIES)
    )
    head_rows = lax.all_to_all(attended_output, "kv", split_axis=1, concat_axis=0, tiled=True)
    picked = head_rows
    projected = lax.psum_scatter(
        jnp.dot(picked, out_weight, preferred_element_type=jnp.float32).astype(jnp.bfloat16),
        "kv",
        scatter_dimension=0,
        tiled=True,
    ).astype(jnp.float32)
    stream = (residual.astype(jnp.float32) + rms_scale(projected, attn_gain)).astype(jnp.bfloat16)
    normed = rms_scale(stream.astype(jnp.float32), pre_gain).astype(jnp.bfloat16)
    row_order = jnp.argsort(regroup)
    destination_rows = regroup[row_order]
    sorted_normed = normed[row_order]
    sorted_stream = stream[row_order]
    sorted_keys = keys[row_order]
    sorted_values = values[row_order]
    received = send_rows(
        sorted_normed, destination_rows % resident_rows, sorted_stream, sorted_keys, sorted_values
    )
    placed = jnp.argsort(received[1])
    own_normed = received[0][placed]
    group_normed = lax.all_gather(own_normed, "kv", axis=0, tiled=True)
    own_stream = received[2][placed]
    resident_keys = received[3][placed]
    resident_values = received[4][placed]
    picked = group_normed
    gate_part = jnp.dot(picked, gate_weight, preferred_element_type=jnp.float32)
    up_part = jnp.dot(picked, up_weight, preferred_element_type=jnp.float32)
    active = (jax.nn.gelu(gate_part, approximate=True) * up_part).astype(jnp.bfloat16)
    ffw_sum = lax.psum_scatter(
        jnp.dot(active, down_weight, preferred_element_type=jnp.float32).astype(jnp.bfloat16),
        "kv",
        scatter_dimension=0,
        tiled=True,
    ).astype(jnp.float32)
    layer_out = (own_stream.astype(jnp.float32) + rms_scale(ffw_sum, post_gain)).astype(
        jnp.bfloat16
    )
    key_cache_rows = resident_keys.reshape(resident_rows, KEY_VALUE_HEADS, HEAD_ENTRIES).transpose(
        1, 0, 2
    )
    value_cache_rows = resident_values.reshape(
        resident_rows, KEY_VALUE_HEADS, HEAD_ENTRIES
    ).transpose(1, 0, 2)
    return (layer_out, key_cache_rows, value_cache_rows)


def solution(mesh):
    placed = (
        P(("req", "kv"), None),
        P(("req", "kv"), None),
        P(("req", "kv"), None),
        P(("req", "kv"), None),
        P(("req", "kv")),
        P(("req", "kv")),
        P("kv", None),
        P(),
        P(),
        P(None, "kv"),
        P(None, "kv"),
        P("kv", None),
        P(),
    )
    return jax.shard_map(
        per_device,
        mesh=mesh,
        in_specs=placed,
        out_specs=(
            P(("req", "kv"), None),
            P(None, ("req", "kv"), None),
            P(None, ("req", "kv"), None),
        ),
        check_vma=False,
    )
```

profile of v0, /device:TPU:1, one launch (start us, length us, event | category | flops | bytes accessed | tf_op | source)
XLA Modules:
  0.0 216.2 jit_solution(5172984267959892114)
XLA Ops:
  17.9 4.2 %all_to_all.76 = bf16[128,2,1024]{2,0,1:T(8,128)(2,1)S(1)} all-to-all(bf16[128,2,1024]{2,0,1:T(8,128)(2,1)S(1)} %copy.50), channel_id=1, replica_groups=mesh['req'=64,'kv'=2] {'kv'}, dimensions={1} | all-to-all | bytes 1048576 | tf_op jit(solution)/shard_map/all_to_all | solution.py:96
  22.1 6.4 %convolution_convert_fusion.1 = bf16[256,3584]{1,0:T(8,128)(2,1)} fusion(bf16[256,1024]{1,0:T(8,128)(2,1)S(1)} %bitcast.76, bf16[1024,3584]{1,0:T(8,128)(2,1)} %param.19), kind=kOutput, calls=%fused_computation.13 | convolution fusion | flops 1879965696 | bytes 9699328 | tf_op jit(solution)/shard_map/dot_general | solution.py:99
  29.2 2.5 %sort.31 = (s32[128]{0:T(128)}, s32[128]{0:T(128)S(1)}) sort(s32[128]{0:T(128)S(1)} %copy-done, s32[128]{0:T(128)S(1)} %iota.18), dimensions={0}, to_apply=%region_3.4 | sort | flops 896 | bytes 2048 | tf_op jit(solution)/shard_map/jit(argsort)/sort | solution.py:106
  33.8 10.9 %all-to-all-start.2 = ((s32[128,1,1]{2,1,0:T(1,128)}), s32[128,1,1]{2,1,0:T(1,128)S(1)}, u32[]{:S(2)}, u32[]{:S(2)}) async-start(s32[128,1,1]{2,1,0:T(1,128)} %copy.52), calls=%async_computation.3 | async-start | bytes 131072 | tf_op jit(solution)/shard_map/all_to_all | solution.py:49
  46.2 1.8 fusion.12
  52.2 2.0 all-to-all-done.2
  54.2 7.8 %all-to-all-start.3 = ((bf16[128,2,1792]{2,1,0:T(2,128)(2,1)}), bf16[128,2,1792]{2,1,0:T(2,128)(2,1)S(1)}, u32[]{:S(2)}, u32[]{:S(2)}) async-start(bf16[128,2,1792]{2,1,0:T(2,128)(2,1)} %reshape.194), calls=%async_computation.4 | async-start | bytes 1835008 | tf_op jit(solution)/shard_map/all_to_all | solution.py:48
  62.0 2.4 %reduce = s32[128]{0:T(128)S(1)} reduce(s32[128,1,1]{2,1,0:T(1,128)S(1)} %all-to-all-done.2, s32[]{:T(128)} %constant.17.clone.1), dimensions={1,2}, to_apply=%all_to_all.59.reduce_sub_computation | reduce | bytes 1028 | tf_op jit(solution)/shard_map/all_to_all | solution.py:49
  64.4 2.5 %sort.32 = (s32[128]{0:T(128)}, s32[128]{0:T(128)S(1)}) sort(s32[128]{0:T(128)S(1)} %reduce, s32[128]{0:T(128)S(1)} %iota.19), dimensions={0}, to_apply=%region_4.5 | sort | flops 896 | bytes 2048 | tf_op jit(solution)/shard_map/jit(argsort)/sort | solution.py:115
  67.0 13.0 %all-to-all-done.3 = bf16[128,2,1792]{2,1,0:T(2,128)(2,1)S(1)} async-done(((bf16[128,2,1792]{2,1,0:T(2,128)(2,1)}), bf16[128,2,1792]{2,1,0:T(2,128)(2,1)S(1)}, u32[]{:S(2)}, u32[]{:S(2)}) %all-to-all-start.3) | async-done | bytes 917536 | tf_op jit(solution)/shard_map/all_to_all | solution.py:48
  79.9 2.1 reshape.195
  82.0 1.6 copy.79
  83.7 2.0 gather_fusion.4
  86.0 9.3 %all-gather.3.cloned.1.call-done = bf16[256,3584]{1,0:T(8,128)(2,1)} async-done(((bf16[128,3584]{1,0:T(8,128)(2,1)}), bf16[256,3584]{1,0:T(8,128)(2,1)}) %all-gather.3.cloned.1.call-update) | async-done | bytes 1835024 | tf_op jit(solution)/shard_map/all_gather | solution.py:117
  95.3 17.1 %fusion.43 = f32[256,3584]{1,0:T(8,128)} fusion(bf16[256,3584]{1,0:T(8,128)(2,1)} %all-gather.3.cloned.1.call-done, bf16[3584,3584]{1,0:T(8,128)(2,1)} %param.22), kind=kOutput, calls=%fused_computation.86 | convolution fusion | flops 6576668672 | bytes 31195136 | tf_op jit(solution)/shard_map/dot_general | solution.py:122
  112.4 24.6 %convolution_convert_fusion = bf16[256,3584]{1,0:T(8,128)(2,1)} fusion(bf16[3584,3584]{1,0:T(8,128)(2,1)} %param.24, bf16[256,3584]{1,0:T(8,128)(2,1)S(1)} %copy-done.7, bf16[3584,3584]{1,0:T(8,128)(2,1)} %param.23, f32[256,3584]{1,0:T(8,128)} %fusion.43), kind=kOutput, calls=%fused_computation.12 | convolution fusion | flops 13163429888 | bytes 58720256 | tf_op jit(solution)/shard_map/dot_general | solution.py:126
  140.3 9.2 %all-to-all-start.4 = ((bf16[128,2,512]{2,1,0:T(2,128)(2,1)}), bf16[128,2,512]{2,1,0:T(2,128)(2,1)S(1)}, u32[]{:S(2)}, u32[]{:S(2)}) async-start(bf16[128,2,512]{2,1,0:T(2,128)(2,1)} %reshape.198), calls=%async_computation.6 | async-start | bytes 524288 | tf_op jit(solution)/shard_map/all_to_all | solution.py:51
  152.0 8.7 %all-to-all-done.4 = bf16[128,2,512]{2,1,0:T(2,128)(2,1)S(1)} async-done(((bf16[128,2,512]{2,1,0:T(2,128)(2,1)}), bf16[128,2,512]{2,1,0:T(2,128)(2,1)S(1)}, u32[]{:S(2)}, u32[]{:S(2)}) %all-to-all-start.4) | async-done | bytes 262176 | tf_op jit(solution)/shard_map/all_to_all | solution.py:51
  160.6 4.4 %all-to-all-start.5 = ((bf16[128,2,512]{2,1,0:T(2,128)(2,1)}), bf16[128,2,512]{2,1,0:T(2,128)(2,1)S(1)}, u32[]{:S(2)}, u32[]{:S(2)}) async-start(bf16[128,2,512]{2,1,0:T(2,128)(2,1)} %reshape.200), calls=%async_computation.7 | async-start | bytes 524288 | tf_op jit(solution)/shard_map/all_to_all | solution.py:52
  168.5 7.6 %all-to-all-done.5 = bf16[128,2,512]{2,1,0:T(2,128)(2,1)S(1)} async-done(((bf16[128,2,512]{2,1,0:T(2,128)(2,1)}), bf16[128,2,512]{2,1,0:T(2,128)(2,1)S(1)}, u32[]{:S(2)}, u32[]{:S(2)}) %all-to-all-start.5) | async-done | bytes 262176 | tf_op jit(solution)/shard_map/all_to_all | solution.py:52
  176.1 5.1 %all-to-all-start.1 = ((bf16[128,2,1792]{2,1,0:T(2,128)(2,1)}), bf16[128,2,1792]{2,1,0:T(2,128)(2,1)}, u32[]{:S(2)}, u32[]{:S(2)}) async-start(bf16[128,2,1792]{2,1,0:T(2,128)(2,1)} %reshape.196), calls=%async_computation.2 | async-start | bytes 1835008 | tf_op jit(solution)/shard_map/all_to_all | solution.py:50
  184.5 14.5 %all-to-all-done.1 = bf16[128,2,1792]{2,1,0:T(2,128)(2,1)} async-done(((bf16[128,2,1792]{2,1,0:T(2,128)(2,1)}), bf16[128,2,1792]{2,1,0:T(2,128)(2,1)}, u32[]{:S(2)}, u32[]{:S(2)}) %all-to-all-start.1) | async-done | bytes 917536 | tf_op jit(solution)/shard_map/all_to_all | solution.py:50
  199.0 5.4 %reshape.197 = bf16[128,1,3584]{2,1,0:T(2,128)(2,1)S(1)} reshape(bf16[128,2,1792]{2,1,0:T(2,128)(2,1)} %all-to-all-done.1) | data formatting | bytes 1835008
  207.2 2.5 %fusion.18 = bf16[128,3584]{1,0:T(8,128)(2,1)} fusion(bf16[128,3584]{1,0:T(8,128)(2,1)} %reduce-scatter.5.cloned.1.call-done, bf16[128,3584]{1,0:T(8,128)(2,1)S(1)} %gather_fusion.2, f32[3584]{0:T(1024)S(1)} %copy-done.6, f32[128]{0:T(128)S(1)} %add_rsqrt_fusion), kind=kLoop, calls=%fused_computation.37 | loop fusion | flops 2752512 | bytes 2767360 | tf_op jit(solution)/shard_map/convert_element_type | solution.py:131
  (81 shorter events, 34.4 us)
Async XLA Ops:
  7.2 37.5 %reduce-scatter.3.cloned.1.call-start = ((), (), s32[]{:S(2)}) async-start(), calls=%async_computation.8 | async-start | bytes 2752512 | tf_op jit(solution)/shard_map/reduce_scatter | solution.py:98
  7.9 6.5 %collective-permute-start.1 = (s32[128]{0:T(128)S(1)}, s32[128]{0:T(128)S(1)}, u32[]{:S(2)}, u32[]{:S(2)}) collective-permute-start(s32[128]{0:T(128)S(1)} %broadcast_add_fusion), channel_id=1, source_target_pairs={{0,1},{2,3},{4,5},{6,7},{8,9},{10,11},{12,13},{14,15},{16,17},{18,... | collective-permute-start | bytes 1544 | tf_op jit(solution)/shard_map/ppermute | solution.py:17
  10.3 6.4 %collective-permute-start.2 = (bf16[128,1024]{0,1:T(8,128)(2,1)S(1)}, bf16[128,1024]{0,1:T(8,128)(2,1)S(1)}, u32[]{:S(2)}, u32[]{:S(2)}) collective-permute-start(bf16[128,1024]{0,1:T(8,128)(2,1)S(1)} %copy.46), channel_id=1, source_target_pairs={{0,1},{2,3},{4,5},{6,7},{8,9},{10,11},{12,13},{14,15},{16,17},{18,... | collective-permute-start | bytes 786440 | tf_op jit(solution)/shard_map/ppermute | solution.py:17
  11.6 4.0 %collective-permute-start = (bf16[128,1024]{1,0:T(8,128)(2,1)}, bf16[128,1024]{1,0:T(8,128)(2,1)S(1)}, u32[]{:S(2)}, u32[]{:S(2)}) collective-permute-start(bf16[128,1024]{1,0:T(8,128)(2,1)} %param.15), channel_id=1, source_target_pairs={{0,1},{2,3},{4,5},{6,7},{8,9},{10,11},{12,13},{14,15},{16,17},{18,... | collective-permute-start | bytes 786440 | tf_op jit(solution)/shard_map/ppermute | solution.py:17
  28.6 0.7 copy-start
  28.6 17.6 %copy-start.3 = (bf16[128,3584]{1,0:T(8,128)(2,1)S(1)}, bf16[128,3584]{1,0:T(8,128)(2,1)}, u32[]{:S(2)}) copy-start(bf16[128,3584]{1,0:T(8,128)(2,1)} %param.16) | copy-start | bytes 2752516
  28.6 17.6 %copy-start.4 = (f32[3584]{0:T(1024)S(1)}, f32[3584]{0:T(1024)}, u32[]{:S(2)}) copy-start(f32[3584]{0:T(1024)} %param.20) | copy-start | bytes 43012
  33.8 20.4 %all-to-all-start.2 = ((s32[128,1,1]{2,1,0:T(1,128)}), s32[128,1,1]{2,1,0:T(1,128)S(1)}, u32[]{:S(2)}, u32[]{:S(2)}) async-start(s32[128,1,1]{2,1,0:T(1,128)} %copy.52), calls=%async_computation.3 | async-start | bytes 131072 | tf_op jit(solution)/shard_map/all_to_all | solution.py:49
  44.7 3.3 %copy-start.5 = (f32[3584]{0:T(1024)S(1)}, f32[3584]{0:T(1024)}, u32[]{:S(2)}) copy-start(f32[3584]{0:T(1024)} %param.21) | copy-start | bytes 43012
  54.2 25.8 %all-to-all-start.3 = ((bf16[128,2,1792]{2,1,0:T(2,128)(2,1)}), bf16[128,2,1792]{2,1,0:T(2,128)(2,1)S(1)}, u32[]{:S(2)}, u32[]{:S(2)}) async-start(bf16[128,2,1792]{2,1,0:T(2,128)(2,1)} %reshape.194), calls=%async_computation.4 | async-start | bytes 1835008 | tf_op jit(solution)/shard_map/all_to_all | solution.py:48
  62.0 33.3 %all-gather.3.cloned.1.call-start = ((), (), s32[]{:S(2)}) async-start(), calls=%async_computation.10 | async-start | bytes 2752512 | tf_op jit(solution)/shard_map/all_gather | solution.py:117
  85.7 120.0 %reduce-scatter.5.cloned.1.call-start = ((), (), s32[]{:S(2)}) async-start(), calls=%async_computation.9 | async-start | bytes 2752512 | tf_op jit(solution)/shard_map/reduce_scatter | solution.py:125
  95.3 17.1 %copy-start.7 = (bf16[256,3584]{1,0:T(8,128)(2,1)S(1)}, bf16[256,3584]{1,0:T(8,128)(2,1)}, u32[]{:S(2)}) copy-start(bf16[256,3584]{1,0:T(8,128)(2,1)} %all-gather.3.cloned.1.call-done) | copy-start | bytes 5505028
  136.9 0.9 copy-start.1
  137.9 11.6 %copy-start.2 = (bf16[128,1024]{1,0:T(8,128)(2,1)S(1)}, bf16[128,1024]{1,0:T(8,128)(2,1)}, u32[]{:S(2)}) copy-start(bf16[128,1024]{1,0:T(8,128)(2,1)} %param.15) | copy-start | bytes 786436
  140.3 20.3 %all-to-all-start.4 = ((bf16[128,2,512]{2,1,0:T(2,128)(2,1)}), bf16[128,2,512]{2,1,0:T(2,128)(2,1)S(1)}, u32[]{:S(2)}, u32[]{:S(2)}) async-start(bf16[128,2,512]{2,1,0:T(2,128)(2,1)} %reshape.198), calls=%async_computation.6 | async-start | bytes 524288 | tf_op jit(solution)/shard_map/all_to_all | solution.py:51
  160.6 15.5 %all-to-all-start.5 = ((bf16[128,2,512]{2,1,0:T(2,128)(2,1)}), bf16[128,2,512]{2,1,0:T(2,128)(2,1)S(1)}, u32[]{:S(2)}, u32[]{:S(2)}) async-start(bf16[128,2,512]{2,1,0:T(2,128)(2,1)} %reshape.200), calls=%async_computation.7 | async-start | bytes 524288 | tf_op jit(solution)/shard_map/all_to_all | solution.py:52
  176.1 22.9 %all-to-all-start.1 = ((bf16[128,2,1792]{2,1,0:T(2,128)(2,1)}), bf16[128,2,1792]{2,1,0:T(2,128)(2,1)}, u32[]{:S(2)}, u32[]{:S(2)}) async-start(bf16[128,2,1792]{2,1,0:T(2,128)(2,1)} %reshape.196), calls=%async_computation.2 | async-start | bytes 1835008 | tf_op jit(solution)/shard_map/all_to_all | solution.py:50
  204.6 2.6 %copy-start.6 = (f32[3584]{0:T(1024)S(1)}, f32[3584]{0:T(1024)}, u32[]{:S(2)}) copy-start(f32[3584]{0:T(1024)} %param.25) | copy-start | bytes 43012
Sparse Core Ops, SparseCore 0:
  28.7 15.0 reduce-scatter.2
  85.9 9.4 all-gather.2
  137.1 13.3 reduce-scatter.4
where the time goes:
time: 217 us; the launch traced here: 216 us
  waiting for transfers between devices  56.2 us (26%)
  matrix products  48.9 us (23%)
  starting transfers between devices  41.6 us (19%)
  local copies, waits for them, and re-layouts  30.5 us (14%)
  other arithmetic  20.6 us (9%)
  between operations  14.1 us (6%)
  blocking collectives  4.22 us (2%)
    dot_general x1, matrix products, per_device(): jnp.dot(active, down_weight, preferred_element_type=jnp.float32)  24.6 us
    dot_general x1, matrix products, per_device(): gate_part = jnp.dot(picked, gate_weight, preferred_element_type=jnp.float32)  17.1 us
    unnamed x29, local copies, waits for them, and re-layouts  16.6 us
    all_to_all x1, waiting for transfers between devices, send_rows(): lax.all_to_all(stream_part, ('req', 'kv'), split_axis=0, concat_axis=0, t...  14.5 us
    all_to_all x1, waiting for transfers between devices, send_rows(): lax.all_to_all(normed_part, ('req', 'kv'), split_axis=0, concat_axis=0, t...  13 us
    all_to_all x1, starting transfers between devices, send_rows(): lax.all_to_all(normed_pos, ('req', 'kv'), split_axis=0, concat_axis=0, ti...  10.9 us
    all_gather x1, waiting for transfers between devices, per_device(): group_normed = lax.all_gather(own_normed, 'kv', axis=0, tiled=True)  9.35 us
    all_to_all x1, starting transfers between devices, send_rows(): lax.all_to_all(key_portion, ('req', 'kv'), split_axis=0, concat_axis=0, t...  9.19 us
  transfers between devices with their start and end apart: 11, of which 7 were waited for; matrix products, arithmetic and copies ran while one was open for 18% of the time, Pallas kernels for 0%

commit v1 on v0

--- a/solution.py
+++ b/solution.py
@@ -114,7 +114,10 @@
     )
     placed = jnp.argsort(received[1])
     own_normed = received[0][placed]
-    group_normed = lax.all_gather(own_normed, "kv", axis=0, tiled=True)
+    local_part = jnp.concatenate(lax.axis_size("kv") * [own_normed], axis=0)
+    group_normed = lax.all_to_all(
+        local_part, axis_name="kv", split_axis=0, concat_axis=0, tiled=True
+    )
     own_stream = received[2][placed]
     resident_keys = received[3][placed]
     resident_values = received[4][placed]

time: 217 us -> 204 us (0.940)
  waiting for transfers between devices: 56.2 us -> 46.9 us
  blocking collectives: 4.22 us -> 9.99 us
  starting transfers between devices: 41.6 us -> 36 us
  matrix products: 48.9 us -> 45.5 us
    all_gather x1 -> x0, waiting for transfers between devices: 9.35 us -> none  [per_device(): group_normed = lax.all_gather(own_normed, 'kv', axis=0, tiled=True)]
    all_to_all x0 -> x1, blocking collectives: none -> 5.77 us  [per_device(): lax.all_to_all(local_part, axis_name='kv', split_axis=0, concat_axis=0, t...]
    all_to_all x1, starting transfers between devices: 9.19 us -> 3.82 us  [send_rows(): lax.all_to_all(key_portion, ('req', 'kv'), split_axis=0, concat_axis=0, t...]
    dot_general x1, matrix products: 17.1 us -> 13.7 us  [per_device(): gate_part = jnp.dot(picked, gate_weight, preferred_element_type=jnp.float32)]
    unnamed x29 -> x27, local copies, waits for them, and re-layouts: 16.6 us -> 16.6 us
  transfers between devices with their start and end apart: 11 -> 10, of which waited for: 7 -> 6; matrix products, arithmetic and copies ran while one was open for 18% -> 19% of each run, Pallas kernels for 0% -> 0%
where the time goes in v1:
time: 204 us; the launch traced here: 203 us
  waiting for transfers between devices  46.9 us (23%)
  matrix products  45.5 us (22%)
  starting transfers between devices  36 us (18%)
  local copies, waits for them, and re-layouts  29.6 us (15%)
  other arithmetic  20.7 us (10%)
  between operations  14.4 us (7%)
  blocking collectives  9.99 us (5%)
    dot_general x1, matrix products, per_device(): jnp.dot(active, down_weight, preferred_element_type=jnp.float32)  24.6 us
    unnamed x27, local copies, waits for them, and re-layouts  16.6 us
    all_to_all x1, waiting for transfers between devices, send_rows(): lax.all_to_all(stream_part, ('req', 'kv'), split_axis=0, concat_axis=0, t...  14.5 us
    dot_general x1, matrix products, per_device(): gate_part = jnp.dot(picked, gate_weight, preferred_element_type=jnp.float32)  13.7 us
    all_to_all x1, waiting for transfers between devices, send_rows(): lax.all_to_all(normed_part, ('req', 'kv'), split_axis=0, concat_axis=0, t...  13 us
    all_to_all x1, starting transfers between devices, send_rows(): lax.all_to_all(normed_pos, ('req', 'kv'), split_axis=0, concat_axis=0, ti...  10.9 us
    all_to_all x1, waiting for transfers between devices, send_rows(): lax.all_to_all(key_portion, ('req', 'kv'), split_axis=0, concat_axis=0, t...  8.71 us
    all_to_all x1, starting transfers between devices, send_rows(): lax.all_to_all(normed_part, ('req', 'kv'), split_axis=0, concat_axis=0, t...  7.8 us
  transfers between devices with their start and end apart: 10, of which 6 were waited for; matrix products, arithmetic and copies ran while one was open for 19% of the time, Pallas kernels for 0%

profile of v1, /device:TPU:1, one launch (start us, length us, event | category | flops | bytes accessed | tf_op | source)
XLA Modules:
  0.0 203.2 jit_solution(10153086298071055397)
XLA Ops:
  17.9 4.2 %all_to_all.88 = bf16[128,2,1024]{2,0,1:T(8,128)(2,1)S(1)} all-to-all(bf16[128,2,1024]{2,0,1:T(8,128)(2,1)S(1)} %copy.50), channel_id=1, replica_groups=mesh['req'=64,'kv'=2] {'kv'}, dimensions={1} | all-to-all | bytes 1048576 | tf_op jit(solution)/shard_map/all_to_all | solution.py:96
  22.1 6.4 %convolution_convert_fusion.1 = bf16[256,3584]{1,0:T(8,128)(2,1)} fusion(bf16[256,1024]{1,0:T(8,128)(2,1)S(1)} %bitcast.81, bf16[1024,3584]{1,0:T(8,128)(2,1)} %param.19), kind=kOutput, calls=%fused_computation.13 | convolution fusion | flops 1879965696 | bytes 9699328 | tf_op jit(solution)/shard_map/dot_general | solution.py:99
  29.2 2.5 %sort.31 = (s32[128]{0:T(128)}, s32[128]{0:T(128)S(1)}) sort(s32[128]{0:T(128)S(1)} %copy-done, s32[128]{0:T(128)S(1)} %iota.18), dimensions={0}, to_apply=%region_3.4 | sort | flops 896 | bytes 2048 | tf_op jit(solution)/shard_map/jit(argsort)/sort | solution.py:106
  33.8 10.9 %all-to-all-start.2 = ((s32[128,1,1]{2,1,0:T(1,128)}), s32[128,1,1]{2,1,0:T(1,128)S(1)}, u32[]{:S(2)}, u32[]{:S(2)}) async-start(s32[128,1,1]{2,1,0:T(1,128)} %copy.52), calls=%async_computation.3 | async-start | bytes 131072 | tf_op jit(solution)/shard_map/all_to_all | solution.py:49
  44.7 1.4 fusion.8
  46.2 1.8 fusion.12
  52.2 2.0 all-to-all-done.2
  54.2 7.8 %all-to-all-start.3 = ((bf16[128,2,1792]{2,1,0:T(2,128)(2,1)}), bf16[128,2,1792]{2,1,0:T(2,128)(2,1)S(1)}, u32[]{:S(2)}, u32[]{:S(2)}) async-start(bf16[128,2,1792]{2,1,0:T(2,128)(2,1)} %reshape.195), calls=%async_computation.4 | async-start | bytes 1835008 | tf_op jit(solution)/shard_map/all_to_all | solution.py:48
  62.0 2.4 %reduce = s32[128]{0:T(128)S(1)} reduce(s32[128,1,1]{2,1,0:T(1,128)S(1)} %all-to-all-done.2, s32[]{:T(128)} %constant.17.clone.1), dimensions={1,2}, to_apply=%all_to_all.67.reduce_sub_computation | reduce | bytes 1028 | tf_op jit(solution)/shard_map/all_to_all | solution.py:49
  64.4 2.5 %sort.32 = (s32[128]{0:T(128)}, s32[128]{0:T(128)S(1)}) sort(s32[128]{0:T(128)S(1)} %reduce, s32[128]{0:T(128)S(1)} %iota.19), dimensions={0}, to_apply=%region_4.5 | sort | flops 896 | bytes 2048 | tf_op jit(solution)/shard_map/jit(argsort)/sort | solution.py:115
  67.0 13.0 %all-to-all-done.3 = bf16[128,2,1792]{2,1,0:T(2,128)(2,1)S(1)} async-done(((bf16[128,2,1792]{2,1,0:T(2,128)(2,1)}), bf16[128,2,1792]{2,1,0:T(2,128)(2,1)S(1)}, u32[]{:S(2)}, u32[]{:S(2)}) %all-to-all-start.3) | async-done | bytes 917536 | tf_op jit(solution)/shard_map/all_to_all | solution.py:48
  79.9 2.1 %reshape.196 = bf16[128,1,3584]{2,1,0:T(2,128)(2,1)} reshape(bf16[128,2,1792]{2,1,0:T(2,128)(2,1)S(1)} %all-to-all-done.3) | data formatting | bytes 1835008
  82.0 1.6 copy.79
  84.9 5.8 %all_to_all.89 = bf16[2,128,3584]{2,1,0:T(8,128)(2,1)S(1)} all-to-all(bf16[2,128,3584]{2,1,0:T(8,128)(2,1)S(1)} %bitcast.69), channel_id=1, replica_groups=mesh['req'=64,'kv'=2] {'kv'}, dimensions={0} | all-to-all | bytes 3670016 | tf_op jit(solution)/shard_map/all_to_all | solution.py:118
  90.7 13.7 %fusion.43 = f32[256,3584]{1,0:T(8,128)} fusion(bf16[256,3584]{1,0:T(8,128)(2,1)S(1)} %bitcast.72, bf16[3584,3584]{1,0:T(8,128)(2,1)} %param.22), kind=kOutput, calls=%fused_computation.87 | convolution fusion | flops 6576668672 | bytes 31195136 | tf_op jit(solution)/shard_map/dot_general | solution.py:125
  104.4 24.6 %convolution_convert_fusion = bf16[256,3584]{1,0:T(8,128)(2,1)} fusion(bf16[3584,3584]{1,0:T(8,128)(2,1)} %param.24, bf16[256,3584]{1,0:T(8,128)(2,1)S(1)} %bitcast.73, bf16[3584,3584]{1,0:T(8,128)(2,1)} %param.23, f32[256,3584]{1,0:T(8,128)} %fusion.43), kind=kOutput, calls=%fused_computation.12 | convolution fusion | flops 13163429888 | bytes 58720256 | tf_op jit(solution)/shard_map/dot_general | solution.py:129
  132.3 3.8 %all-to-all-start.5 = ((bf16[128,2,512]{2,1,0:T(2,128)(2,1)}), bf16[128,2,512]{2,1,0:T(2,128)(2,1)S(1)}, u32[]{:S(2)}, u32[]{:S(2)}) async-start(bf16[128,2,512]{2,1,0:T(2,128)(2,1)} %reshape.199), calls=%async_computation.7 | async-start | bytes 524288 | tf_op jit(solution)/shard_map/all_to_all | solution.py:51
  138.6 8.7 %all-to-all-done.5 = bf16[128,2,512]{2,1,0:T(2,128)(2,1)S(1)} async-done(((bf16[128,2,512]{2,1,0:T(2,128)(2,1)}), bf16[128,2,512]{2,1,0:T(2,128)(2,1)S(1)}, u32[]{:S(2)}, u32[]{:S(2)}) %all-to-all-start.5) | async-done | bytes 262176 | tf_op jit(solution)/shard_map/all_to_all | solution.py:51
  147.3 4.4 %all-to-all-start.6 = ((bf16[128,2,512]{2,1,0:T(2,128)(2,1)}), bf16[128,2,512]{2,1,0:T(2,128)(2,1)S(1)}, u32[]{:S(2)}, u32[]{:S(2)}) async-start(bf16[128,2,512]{2,1,0:T(2,128)(2,1)} %reshape.201), calls=%async_computation.8 | async-start | bytes 524288 | tf_op jit(solution)/shard_map/all_to_all | solution.py:52
  155.2 7.6 %all-to-all-done.6 = bf16[128,2,512]{2,1,0:T(2,128)(2,1)S(1)} async-done(((bf16[128,2,512]{2,1,0:T(2,128)(2,1)}), bf16[128,2,512]{2,1,0:T(2,128)(2,1)S(1)}, u32[]{:S(2)}, u32[]{:S(2)}) %all-to-all-start.6) | async-done | bytes 262176 | tf_op jit(solution)/shard_map/all_to_all | solution.py:52
  162.8 5.1 %all-to-all-start.1 = ((bf16[128,2,1792]{2,1,0:T(2,128)(2,1)}), bf16[128,2,1792]{2,1,0:T(2,128)(2,1)}, u32[]{:S(2)}, u32[]{:S(2)}) async-start(bf16[128,2,1792]{2,1,0:T(2,128)(2,1)} %reshape.197), calls=%async_computation.2 | async-start | bytes 1835008 | tf_op jit(solution)/shard_map/all_to_all | solution.py:50
  171.2 14.5 %all-to-all-done.1 = bf16[128,2,1792]{2,1,0:T(2,128)(2,1)} async-done(((bf16[128,2,1792]{2,1,0:T(2,128)(2,1)}), bf16[128,2,1792]{2,1,0:T(2,128)(2,1)}, u32[]{:S(2)}, u32[]{:S(2)}) %all-to-all-start.1) | async-done | bytes 917536 | tf_op jit(solution)/shard_map/all_to_all | solution.py:50
  185.7 5.4 %reshape.198 = bf16[128,1,3584]{2,1,0:T(2,128)(2,1)S(1)} reshape(bf16[128,2,1792]{2,1,0:T(2,128)(2,1)} %all-to-all-done.1) | data formatting | bytes 1835008
  193.9 2.5 %fusion.18 = bf16[128,3584]{1,0:T(8,128)(2,1)} fusion(bf16[128,3584]{1,0:T(8,128)(2,1)} %reduce-scatter.5.cloned.1.call-done, bf16[128,3584]{1,0:T(8,128)(2,1)S(1)} %gather_fusion.2, f32[3584]{0:T(1024)S(1)} %copy-done.6, f32[128]{0:T(128)S(1)} %add_rsqrt_fusion), kind=kLoop, calls=%fused_computation.37 | loop fusion | flops 2752512 | bytes 2767360 | tf_op jit(solution)/shard_map/convert_element_type | solution.py:134
  (78 shorter events, 34.0 us)
Async XLA Ops:
  7.2 37.5 %reduce-scatter.3.cloned.1.call-start = ((), (), s32[]{:S(2)}) async-start(), calls=%async_computation.9 | async-start | bytes 2752512 | tf_op jit(solution)/shard_map/reduce_scatter | solution.py:98
  7.9 6.5 %collective-permute-start.1 = (s32[128]{0:T(128)S(1)}, s32[128]{0:T(128)S(1)}, u32[]{:S(2)}, u32[]{:S(2)}) collective-permute-start(s32[128]{0:T(128)S(1)} %broadcast_add_fusion), channel_id=1, source_target_pairs={{0,1},{2,3},{4,5},{6,7},{8,9},{10,11},{12,13},{14,15},{16,17},{18,... | collective-permute-start | bytes 1544 | tf_op jit(solution)/shard_map/ppermute | solution.py:17
  10.3 6.4 %collective-permute-start.2 = (bf16[128,1024]{0,1:T(8,128)(2,1)S(1)}, bf16[128,1024]{0,1:T(8,128)(2,1)S(1)}, u32[]{:S(2)}, u32[]{:S(2)}) collective-permute-start(bf16[128,1024]{0,1:T(8,128)(2,1)S(1)} %copy.46), channel_id=1, source_target_pairs={{0,1},{2,3},{4,5},{6,7},{8,9},{10,11},{12,13},{14,15},{16,17},{18,... | collective-permute-start | bytes 786440 | tf_op jit(solution)/shard_map/ppermute | solution.py:17
  11.6 4.0 %collective-permute-start = (bf16[128,1024]{1,0:T(8,128)(2,1)}, bf16[128,1024]{1,0:T(8,128)(2,1)S(1)}, u32[]{:S(2)}, u32[]{:S(2)}) collective-permute-start(bf16[128,1024]{1,0:T(8,128)(2,1)} %param.15), channel_id=1, source_target_pairs={{0,1},{2,3},{4,5},{6,7},{8,9},{10,11},{12,13},{14,15},{16,17},{18,... | collective-permute-start | bytes 786440 | tf_op jit(solution)/shard_map/ppermute | solution.py:17
  28.6 0.7 copy-start
  28.6 17.6 %copy-start.3 = (bf16[128,3584]{1,0:T(8,128)(2,1)S(1)}, bf16[128,3584]{1,0:T(8,128)(2,1)}, u32[]{:S(2)}) copy-start(bf16[128,3584]{1,0:T(8,128)(2,1)} %param.16) | copy-start | bytes 2752516
  28.6 17.6 %copy-start.4 = (f32[3584]{0:T(1024)S(1)}, f32[3584]{0:T(1024)}, u32[]{:S(2)}) copy-start(f32[3584]{0:T(1024)} %param.20) | copy-start | bytes 43012
  33.8 20.4 %all-to-all-start.2 = ((s32[128,1,1]{2,1,0:T(1,128)}), s32[128,1,1]{2,1,0:T(1,128)S(1)}, u32[]{:S(2)}, u32[]{:S(2)}) async-start(s32[128,1,1]{2,1,0:T(1,128)} %copy.52), calls=%async_computation.3 | async-start | bytes 131072 | tf_op jit(solution)/shard_map/all_to_all | solution.py:49
  44.7 3.3 %copy-start.5 = (f32[3584]{0:T(1024)S(1)}, f32[3584]{0:T(1024)}, u32[]{:S(2)}) copy-start(f32[3584]{0:T(1024)} %param.21) | copy-start | bytes 43012
  54.2 25.8 %all-to-all-start.3 = ((bf16[128,2,1792]{2,1,0:T(2,128)(2,1)}), bf16[128,2,1792]{2,1,0:T(2,128)(2,1)S(1)}, u32[]{:S(2)}, u32[]{:S(2)}) async-start(bf16[128,2,1792]{2,1,0:T(2,128)(2,1)} %reshape.195), calls=%async_computation.4 | async-start | bytes 1835008 | tf_op jit(solution)/shard_map/all_to_all | solution.py:48
  62.0 130.4 %reduce-scatter.5.cloned.1.call-start = ((), (), s32[]{:S(2)}) async-start(), calls=%async_computation.10 | async-start | bytes 2752512 | tf_op jit(solution)/shard_map/reduce_scatter | solution.py:128
  128.9 0.9 copy-start.1
  129.9 6.3 %copy-start.2 = (bf16[128,1024]{1,0:T(8,128)(2,1)S(1)}, bf16[128,1024]{1,0:T(8,128)(2,1)}, u32[]{:S(2)}) copy-start(bf16[128,1024]{1,0:T(8,128)(2,1)} %param.15) | copy-start | bytes 786436
  132.3 15.0 %all-to-all-start.5 = ((bf16[128,2,512]{2,1,0:T(2,128)(2,1)}), bf16[128,2,512]{2,1,0:T(2,128)(2,1)S(1)}, u32[]{:S(2)}, u32[]{:S(2)}) async-start(bf16[128,2,512]{2,1,0:T(2,128)(2,1)} %reshape.199), calls=%async_computation.7 | async-start | bytes 524288 | tf_op jit(solution)/shard_map/all_to_all | solution.py:51
  147.3 15.5 %all-to-all-start.6 = ((bf16[128,2,512]{2,1,0:T(2,128)(2,1)}), bf16[128,2,512]{2,1,0:T(2,128)(2,1)S(1)}, u32[]{:S(2)}, u32[]{:S(2)}) async-start(bf16[128,2,512]{2,1,0:T(2,128)(2,1)} %reshape.201), calls=%async_computation.8 | async-start | bytes 524288 | tf_op jit(solution)/shard_map/all_to_all | solution.py:52
  162.8 22.9 %all-to-all-start.1 = ((bf16[128,2,1792]{2,1,0:T(2,128)(2,1)}), bf16[128,2,1792]{2,1,0:T(2,128)(2,1)}, u32[]{:S(2)}, u32[]{:S(2)}) async-start(bf16[128,2,1792]{2,1,0:T(2,128)(2,1)} %reshape.197), calls=%async_computation.2 | async-start | bytes 1835008 | tf_op jit(solution)/shard_map/all_to_all | solution.py:50
  191.2 2.6 %copy-start.6 = (f32[3584]{0:T(1024)S(1)}, f32[3584]{0:T(1024)}, u32[]{:S(2)}) copy-start(f32[3584]{0:T(1024)} %param.25) | copy-start | bytes 43012
Sparse Core Ops, SparseCore 0:
  28.7 15.0 reduce-scatter.2
  129.1 7.9 reduce-scatter.4
